TPU v7x, 32 devices: a whole 2x2x4 slice. The times are simulated.
32 devices in a mesh: groups: 2 (over x), seq: 16 (over z, y, core).
Axes of the slice: x: 2, y: 2, z: 4, core: 2. Of those that a mesh axis runs over, the one named last changes fastest.
Arguments:
- latent: bfloat16 [32, 32768], P(('groups', 'seq')), parts along dimension 0, may hold values from -6 to 6
- text_embed: bfloat16 [4, 128, 3072], P('groups'), parts along dimension 0, may hold values from -6 to 6
- text_mask: int32 [4, 128], P('groups'), parts along dimension 0, may hold values from 0 to 1, as said below
- modulation: float32 [4, 5, 3072], P('groups'), parts along dimension 0, may hold values from -3 to 10
- w_in: bfloat16 [64, 3072], replicated, may hold values from -0.75 to 0.75
- w_qkv: bfloat16 [3072, 4608], P(None, 'seq'), may hold values from -0.109375 to 0.109375
- w_attn_out: bfloat16 [1536, 3072], P(None, 'seq'), may hold values from -0.15625 to 0.15625
- w_final: bfloat16 [3072, 64], replicated, may hold values from -0.109375 to 0.109375
Outputs:
- guided: float32 [32, 32768], P(('groups', 'seq')), parts along dimension 0
There are 2 independent parts, one for each index of `groups`. A program takes and returns all parts, laid end to end along the dimension named above; an argument that names none is the same for every part. Nothing has to cross between parts.
Inputs may be any that keep to these rules, and one draw needn't show every extreme that they name: `text_mask`: each row is 1 on a leading run of 1 to 127 positions and 0 after it.
All inputs are finite; a program needn't handle non-finite values.
Results may differ from a plain program's by a relative error of at most 0.007.
The roundings to bfloat16 on the way count: a program that leaves them out, or rounds other values in their place, can miss the bound.
Values may be sent and summed in bfloat16 or wider, within the bound.
A program may use at most 128 MiB of HBM per device.

v0:
```python
import jax
import jax.numpy as jnp
from jax import lax
from jax.sharding import PartitionSpec as P

HDIM = 128
SHEADS = 6
THEADS = 6
CHAN = 64
HEADS = 12
EPS = 1e-06
GUIDE = 5.0


def normalize(values):
    center = values - jnp.mean(values, axis=-1, keepdims=True)
    spread = jnp.mean(center * center, axis=-1, keepdims=True)
    return center * lax.rsqrt(spread + EPS)


def attend(query, keys, values, live):
    scores = jnp.einsum("qhe,khe->hqk", query, keys, preferred_element_type=jnp.float32) * HDIM ** (
        -0.5
    )
    scores = jnp.where(live[None, None, :], scores, -1e30)
    top = jnp.max(scores, axis=-1, keepdims=True)
    weights = jnp.exp(scores - top)
    total = jnp.sum(weights, axis=-1, keepdims=True)
    probs = weights.astype(jnp.bfloat16)
    mixed = jnp.einsum("hqk,khe->qhe", probs, values, preferred_element_type=jnp.float32)
    return (mixed / jnp.transpose(total, (1, 0, 2))).astype(jnp.bfloat16)


def temporal_mix(block):
    frames, span, heads = (block.shape[0], block.shape[1], block.shape[3])
    grid = block.reshape(2, frames // 2, span, 3, heads, HDIM)
    scores = jnp.einsum(
        "afpne,agpne->apnfg", grid[:, :, :, 0], grid[:, :, :, 1], preferred_element_type=jnp.float32
    ) * HDIM ** (-0.5)
    top = jnp.max(scores, axis=-1, keepdims=True)
    weights = jnp.exp(scores - top)
    total = jnp.sum(weights, axis=-1)
    probs = weights.astype(jnp.bfloat16)
    mixed = jnp.einsum(
        "apnfg,agpne->afpne", probs, grid[:, :, :, 2], preferred_element_type=jnp.float32
    )
    mixed = mixed / jnp.moveaxis(total, 3, 1)[..., None]
    return mixed.astype(jnp.bfloat16).reshape(frames, span, heads, HDIM)


def temporal_local(pieces):
    qkv_piece, spatial_piece, latent_piece = pieces
    frames_here, width = (qkv_piece.shape[0], qkv_piece.shape[2])
    mixed = temporal_mix(qkv_piece.reshape(frames_here, width, 3, THEADS, HDIM))
    return (mixed.reshape(frames_here, 1, width, THEADS * HDIM), spatial_piece, latent_piece)


def per_device(latent, text_embed, text_mask, modulation, w_in, w_qkv, w_attn_out, w_final):
    count = lax.axis_size("seq")
    index = lax.axis_index("seq")
    half = index // (count // 2)
    positions = latent.shape[1] // CHAN
    start = jnp.dot(latent.reshape(positions, CHAN), w_in, preferred_element_type=jnp.float32)
    mods = lax.dynamic_index_in_dim(modulation, half, 0, keepdims=False)
    hidden = (normalize(start) * (1.0 + mods[1]) + mods[0]).astype(jnp.bfloat16)
    words = lax.dynamic_index_in_dim(text_embed, half, 0, keepdims=False)
    valid = lax.dynamic_index_in_dim(text_mask, half, 0, keepdims=False) > 0
    rows = jnp.concatenate([hidden, words], axis=0)
    projected = jnp.dot(
        rows, lax.all_gather(w_qkv, "seq", axis=1, tiled=True), preferred_element_type=jnp.float32
    ).astype(jnp.bfloat16)
    projected = projected.reshape(rows.shape[0], 3, HEADS, HDIM)
    live = jnp.concatenate([jnp.ones((positions,), bool), valid])
    spatial_out = attend(
        projected[:positions, 0, :SHEADS], projected[:, 1, :SHEADS], projected[:, 2, :SHEADS], live
    )
    span = positions // count
    temporal_rows = projected[:positions, :, SHEADS:].reshape(1, count, span, 3 * THEADS * HDIM)
    spatial_rows = spatial_out.reshape(1, count, span, SHEADS * HDIM)
    latent_rows = latent.reshape(1, count, span, CHAN)
    temporal_pos, spatial_pos, latent_pos = temporal_local(
        (
            lax.all_to_all(temporal_rows, "seq", split_axis=1, concat_axis=0, tiled=True),
            lax.all_to_all(spatial_rows, "seq", split_axis=1, concat_axis=0, tiled=True),
            lax.all_to_all(latent_rows, "seq", split_axis=1, concat_axis=0, tiled=True),
        )
    )
    joined = jnp.concatenate(
        [
            spatial_pos.reshape(positions, SHEADS * HDIM),
            temporal_pos.reshape(positions, THEADS * HDIM),
        ],
        axis=1,
    )
    mixed_out = jnp.dot(
        joined,
        lax.all_gather(w_attn_out, "seq", axis=1, tiled=True),
        preferred_element_type=jnp.float32,
    )
    cond_side = (jnp.arange(count) < count // 2)[:, None, None]
    frame_mods = jnp.where(cond_side, modulation[0][None], modulation[1][None])
    start_here = jnp.dot(
        latent_pos.reshape(positions, CHAN), w_in, preferred_element_type=jnp.float32
    )
    block = start_here.reshape(count, span, -1) + frame_mods[:, 2][:, None, :] * mixed_out.reshape(
        count, span, -1
    )
    final = (
        normalize(block) * (1.0 + frame_mods[:, 4][:, None, :]) + frame_mods[:, 3][:, None, :]
    ).astype(jnp.bfloat16)
    pred = jnp.dot(
        final.reshape(positions, -1), w_final, preferred_element_type=jnp.float32
    ).astype(jnp.bfloat16)
    pred = lax.optimization_barrier(pred).astype(jnp.float32).reshape(count, span, CHAN)
    cond_pred = pred[: count // 2]
    uncond_pred = pred[count // 2 :]
    guided_here = uncond_pred + GUIDE * (cond_pred - uncond_pred)
    both_halves = jnp.concatenate([guided_here, guided_here], axis=0)
    result = lax.all_to_all(
        both_halves.astype(jnp.bfloat16), "seq", split_axis=0, concat_axis=1, tiled=True
    ).astype(both_halves.dtype)
    return result.reshape(1, positions * CHAN)


def solution(mesh):
    in_specs = (
        P(("groups", "seq"), None),
        P("groups", None, None),
        P("groups", None),
        P("groups", None, None),
        P(),
        P(None, "seq"),
        P(None, "seq"),
        P(),
    )
    out_specs = P(("groups", "seq"), None)
    return jax.shard_map(
        per_device, mesh=mesh, in_specs=in_specs, out_specs=out_specs, check_vma=False
    )
```

profile of v0, /device:TPU:0, one launch (start us, length us, event | category | flops | bytes accessed | tf_op | source)
XLA Modules:
  0.0 340.8 jit_solution(5030938691249247104)
XLA Ops:
  8.0 1.3 reduce
  9.4 0.8 reshape.119
  10.2 7.4 %all-to-all-start = ((bf16[16,2,1024]{2,1,0:T(2,128)(2,1)}), bf16[16,2,1024]{2,1,0:T(2,128)(2,1)S(1)}, u32[]{:S(2)}, u32[]{:S(2)}) async-start(bf16[16,2,1024]{2,1,0:T(2,128)(2,1)} %reshape.119), calls=%async_computation | async-start | bytes 131072 | tf_op jit(solution)/shard_map/all_to_all | solution.py:85
  17.7 2.2 fusion.35
  19.9 0.8 multiply_reduce_fusion.1
  20.8 3.3 add_convert_fusion.1
  24.1 132.0 %all-gather.3.cloned.1.call-done = bf16[3072,4608]{0,1:T(8,128)(2,1)} async-done(((bf16[3072,288]{0,1:T(8,128)(2,1)}), bf16[3072,4608]{0,1:T(8,128)(2,1)}) %all-gather.3.cloned.1.call-update) | async-done | bytes 28311568 | tf_op jit(solution)/shard_map/all_gather | solution.py:70
  156.1 24.7 %convolution_convert_fusion = bf16[640,4608]{1,0:T(8,128)(2,1)} fusion(bf16[3072,4608]{0,1:T(8,128)(2,1)} %all-gather.3.cloned.1.call-done, bf16[128,3072]{1,0:T(8,128)(2,1)S(1)} %dynamic-slice_bitcast_fusion, bf16[512,3072]{1,0:T(8,128)(2,1)} %add_convert_fusion.1), kind=kOutput, calls=%fused_computation | convolution fusion | flops 18130206720 | bytes 38141952 | tf_op jit(solution)/shard_map/dot_general | solution.py:69
  180.8 8.9 %copy.30 = bf16[640,4608]{0,1:T(8,128)(2,1)} copy(bf16[640,4608]{1,0:T(8,128)(2,1)} %convolution_convert_fusion) | data formatting | bytes 11796480 | tf_op jit(solution)/shard_map/convert_element_type | solution.py:71
  189.8 3.3 slice.78
  193.1 4.7 %copy.35 = bf16[512,3,6,128]{3,2,1,0:T(8,128)(2,1)} copy(bf16[512,3,6,128]{0,3,2,1:T(8,128)(2,1)} %slice.78) | data formatting | bytes 4718592 | tf_op jit(solution)/shard_map/slice | solution.py:78
  197.8 6.0 %reshape.112 = bf16[1,16,32,2304]{3,2,1,0:T(8,128)(2,1)} reshape(bf16[512,3,6,128]{3,2,1,0:T(8,128)(2,1)} %copy.35) | data formatting | bytes 4718592 | tf_op jit(solution)/shard_map/reshape | solution.py:78
  203.8 4.9 %all-to-all-start.2 = ((bf16[1,16,32,2304]{3,2,0,1:T(8,128)(2,1)}), bf16[1,16,32,2304]{3,2,0,1:T(8,128)(2,1)}, u32[]{:S(2)}, u32[]{:S(2)}) async-start(bf16[1,16,32,2304]{3,2,0,1:T(8,128)(2,1)} %bitcast.101), calls=%async_computation.2 | async-start | bytes 4718592 | tf_op jit(solution)/shard_map/all_to_all | solution.py:83
  209.0 3.0 fusion
  212.1 2.0 fusion.1
  214.1 3.5 %fusion.17 = bf16[512,6,128]{0,2,1:T(8,128)(2,1)S(1)} fusion(f32[6,512,640]{2,1,0:T(8,128)S(1)} %get-tuple-element.22, f32[6,512]{1,0:T(8,128)S(1)} %get-tuple-element.21, pred[640]{0:T(1024)(128)(4,1)S(1)} %concatenate.14, bf16[640,3,12,128]{0,3,2,1:T(8,128)(2,1)} %bitcast.99, f32[512,6]{0,1:T(8,128)S(1)} %bitcast.112), kind=kOutput, calls=%fused_computation.26 | convolution fusion | flops 511967232 | bytes 9659008 | tf_op jit(solution)/shard_map/hqk,khe->qhe/dot_general | solution.py:30
  218.4 1.8 reshape.110
  220.2 56.8 %all-to-all-done.2 = bf16[1,16,32,2304]{3,2,0,1:T(8,128)(2,1)} async-done(((bf16[1,16,32,2304]{3,2,0,1:T(8,128)(2,1)}), bf16[1,16,32,2304]{3,2,0,1:T(8,128)(2,1)}, u32[]{:S(2)}, u32[]{:S(2)}) %all-to-all-start.2) | async-done | bytes 2359328 | tf_op jit(solution)/shard_map/all_to_all | solution.py:83
  277.0 12.3 %all-to-all-start.1 = ((bf16[1,16,32,768]{3,2,0,1:T(8,128)(2,1)}), bf16[1,16,32,768]{3,2,0,1:T(8,128)(2,1)S(1)}, u32[]{:S(2)}, u32[]{:S(2)}) async-start(bf16[1,16,32,768]{3,2,0,1:T(8,128)(2,1)} %bitcast.17), calls=%async_computation.1 | async-start | bytes 1572864 | tf_op jit(solution)/shard_map/all_to_all | solution.py:84
  289.3 0.8 fusion.26
  290.1 0.8 reshape.120
  290.9 6.0 %reshape_reshape.3 = bf16[2,8,32,3,6,128]{5,4,3,2,1,0:T(8,128)(2,1)} reshape(bf16[1,16,32,2304]{3,2,0,1:T(8,128)(2,1)} %all-to-all-done.2) | data formatting | bytes 4718592 | tf_op jit(solution)/shard_map/reshape;reshape | solution.py:36
  296.9 2.4 fusion.32
  299.3 1.3 fusion.36
  301.3 1.1 fusion.16
  302.8 5.2 %all-to-all-done.1 = bf16[1,16,32,768]{3,2,0,1:T(8,128)(2,1)S(1)} async-done(((bf16[1,16,32,768]{3,2,0,1:T(8,128)(2,1)}), bf16[1,16,32,768]{3,2,0,1:T(8,128)(2,1)S(1)}, u32[]{:S(2)}, u32[]{:S(2)}) %all-to-all-start.1) | async-done | bytes 786464 | tf_op jit(solution)/shard_map/all_to_all | solution.py:84
  308.0 7.7 %fusion.12 = f32[512,3072]{1,0:T(8,128)S(1)} fusion(bf16[1536,3072]{0,1:T(8,128)(2,1)} %all-gather.5.cloned.1.call-done, bf16[512,768]{1,0:T(8,128)(2,1)S(1)} %bitcast.104, bf16[512,768]{1,0:T(8,128)(2,1)S(1)} %bitcast.105), kind=kOutput, calls=%fused_computation.19 | convolution fusion | flops 4834983936 | bytes 17301504 | tf_op jit(solution)/shard_map/dot_general | solution.py:95
  315.7 1.0 fusion.37
  317.7 1.6 add_convert_fusion
  319.4 1.1 convolution_convert_fusion.1
  320.9 12.1 %all_to_all.16 = bf16[16,2,1024]{2,1,0:T(2,128)(2,1)S(1)} all-to-all(bf16[16,2,1024]{2,1,0:T(2,128)(2,1)S(1)} %reshape.121), channel_id=1, replica_groups=mesh['groups'=2,'seq'=16] {'seq'}, dimensions={0} | all-to-all | bytes 131072 | tf_op jit(solution)/shard_map/all_to_all | solution.py:119
  333.1 0.9 reshape.115
  (54 shorter events, 5.3 us)
Async XLA Ops:
  6.5 14.2 %copy-start = (bf16[2,128,3072]{2,1,0:T(8,128)(2,1)S(1)}, bf16[2,128,3072]{2,1,0:T(8,128)(2,1)}, u32[]{:S(2)}) copy-start(bf16[2,128,3072]{2,1,0:T(8,128)(2,1)} %param.9) | copy-start | bytes 4718596
  6.5 149.5 %all-gather.3.cloned.1.call-start = ((), (), s32[]{:S(2)}) async-start(), calls=%async_computation.4 | async-start | bytes 30081024 | tf_op jit(solution)/shard_map/all_gather | solution.py:70
  7.3 295.6 %all-gather.5.cloned.1.call-start = ((), (), s32[]{:S(2)}) async-start(), calls=%async_computation.5 | async-start | bytes 10027008 | tf_op jit(solution)/shard_map/all_gather | solution.py:97
  10.2 193.6 %all-to-all-start = ((bf16[16,2,1024]{2,1,0:T(2,128)(2,1)}), bf16[16,2,1024]{2,1,0:T(2,128)(2,1)S(1)}, u32[]{:S(2)}, u32[]{:S(2)}) async-start(bf16[16,2,1024]{2,1,0:T(2,128)(2,1)} %reshape.119), calls=%async_computation | async-start | bytes 131072 | tf_op jit(solution)/shard_map/all_to_all | solution.py:85
  17.7 3.0 copy-start.9
  197.8 10.9 %copy-start.10 = (s32[2,128]{1,0:T(2,128)S(1)}, s32[2,128]{1,0:T(2,128)}, u32[]{:S(2)}) copy-start(s32[2,128]{1,0:T(2,128)} %param.10) | copy-start | bytes 3076
  203.8 5.1 %copy-start.7 = (bf16[16,2,1024]{2,1,0:T(2,128)(2,1)}, bf16[16,2,1024]{2,1,0:T(2,128)(2,1)S(1)}, u32[]{:S(2)}) copy-start(bf16[16,2,1024]{2,1,0:T(2,128)(2,1)S(1)} %all-to-all-done) | copy-start | bytes 196612
  203.8 73.2 %all-to-all-start.2 = ((bf16[1,16,32,2304]{3,2,0,1:T(8,128)(2,1)}), bf16[1,16,32,2304]{3,2,0,1:T(8,128)(2,1)}, u32[]{:S(2)}, u32[]{:S(2)}) async-start(bf16[1,16,32,2304]{3,2,0,1:T(8,128)(2,1)} %bitcast.101), calls=%async_computation.2 | async-start | bytes 4718592 | tf_op jit(solution)/shard_map/all_to_all | solution.py:83
  217.6 72.5 %copy-start.8 = (bf16[16,2,1024]{2,1,0:T(2,128)(2,1)S(1)}, bf16[16,2,1024]{2,1,0:T(2,128)(2,1)}, u32[]{:S(2)}) copy-start(bf16[16,2,1024]{2,1,0:T(2,128)(2,1)} %copy-done.7) | copy-start | bytes 196612
  277.0 31.0 %all-to-all-start.1 = ((bf16[1,16,32,768]{3,2,0,1:T(8,128)(2,1)}), bf16[1,16,32,768]{3,2,0,1:T(8,128)(2,1)S(1)}, u32[]{:S(2)}, u32[]{:S(2)}) async-start(bf16[1,16,32,768]{3,2,0,1:T(8,128)(2,1)} %bitcast.17), calls=%async_computation.1 | async-start | bytes 1572864 | tf_op jit(solution)/shard_map/all_to_all | solution.py:84
  308.0 7.7 %copy-start.2 = (bf16[64,3072]{1,0:T(8,128)(2,1)S(1)}, bf16[64,3072]{1,0:T(8,128)(2,1)}, u32[]{:S(2)}) copy-start(bf16[64,3072]{1,0:T(8,128)(2,1)} %param.12) | copy-start | bytes 1179652
  308.0 7.7 %copy-start.4 = (f32[16,3072]{1,0:T(8,128)S(1)}, f32[16,3072]{1,0:T(8,128)}, u32[]{:S(2)}) copy-start(f32[16,3072]{1,0:T(8,128)} %get-tuple-element.10) | copy-start | bytes 589828
  308.0 7.7 %copy-start.5 = (bf16[16,1,32,64]{3,2,1,0:T(8,128)(2,1)S(1)}, bf16[16,1,32,64]{3,2,1,0:T(8,128)(2,1)}, u32[]{:S(2)}) copy-start(bf16[16,1,32,64]{3,2,1,0:T(8,128)(2,1)} %reshape.120) | copy-start | bytes 196612
  316.8 0.9 copy-start.3
  317.6 1.8 copy-start.6
  317.6 16.4 %copy-start.1 = (bf16[2,128,3072]{2,1,0:T(8,128)(2,1)S(1)}, bf16[2,128,3072]{2,1,0:T(8,128)(2,1)}, u32[]{:S(2)}) copy-start(bf16[2,128,3072]{2,1,0:T(8,128)(2,1)} %param.9) | copy-start | bytes 4718596
Sparse Core Ops, SparseCore 0:
  8.9 147.1 all-gather.2
  158.4 115.3 all-gather.4
where the time goes:
time: 342 us; the launch traced here: 341 us
  waiting for transfers between devices  195 us (57%)
  matrix products  45.7 us (13%)
  local copies, waits for them, and re-layouts  37.8 us (11%)
  starting transfers between devices  24.6 us (7%)
  between operations  13.8 us (4%)
  blocking collectives  12.1 us (4%)
  other arithmetic  11.4 us (3%)
    all_gather x1, waiting for transfers between devices, per_device(): lax.all_gather(w_qkv, 'seq', axis=1, tiled=True)  132 us
    all_to_all x1, waiting for transfers between devices, per_device(): lax.all_to_all(temporal_rows, 'seq', split_axis=1, concat_axis=0, tiled=T...  56.8 us
    dot_general x1, matrix products, per_device(): jnp.dot(rows, lax.all_gather(w_qkv, 'seq', axis=1, tiled=True), preferred...  24.7 us
    all_to_all x1, starting transfers between devices, per_device(): lax.all_to_all(spatial_rows, 'seq', split_axis=1, concat_axis=0, tiled=True)  12.3 us
    all_to_all x1, blocking collectives, per_device(): lax.all_to_all(both_halves.astype(jnp.bfloat16), 'seq', split_axis=0, con...  12.1 us
    convert_element_type x1, local copies, waits for them, and re-layouts, per_device(): projected = jnp.dot(rows, lax.all_gather(w_qkv, 'seq', axis=1, tiled=True...  8.94 us
    slice x2, local copies, waits for them, and re-layouts, per_device(): projected[:positions, :, SHEADS:].reshape(1, count, span, 3 * THEADS * HDIM)  8.03 us
    dot_general x1, matrix products, per_device(): jnp.dot(joined, lax.all_gather(w_attn_out, 'seq', axis=1, tiled=True), pr...  7.7 us
  transfers between devices with their start and end apart: 5, of which 3 were waited for; matrix products, arithmetic and copies ran while one was open for 24% of the time, Pallas kernels for 0%

commit v1 on v0

--- a/solution.py
+++ b/solution.py
@@ -10,6 +10,13 @@
 HEADS = 12
 EPS = 1e-06
 GUIDE = 5.0
+
+
+def swap_blocks(x, name, split, join):
+    devices = lax.axis_size(name)
+    blocks = jnp.stack(jnp.split(x, devices, axis=split), axis=0)
+    blocks = lax.all_to_all(blocks, name, split_axis=0, concat_axis=0)
+    return jnp.concatenate(blocks, axis=join)
 
 
 def normalize(values):
@@ -81,7 +88,7 @@
     temporal_pos, spatial_pos, latent_pos = temporal_local(
         (
             lax.all_to_all(temporal_rows, "seq", split_axis=1, concat_axis=0, tiled=True),
-            lax.all_to_all(spatial_rows, "seq", split_axis=1, concat_axis=0, tiled=True),
+            swap_blocks(spatial_rows, "seq", 1, 0),
             lax.all_to_all(latent_rows, "seq", split_axis=1, concat_axis=0, tiled=True),
         )
     )

time: 342 us -> 342 us (level)
  waiting for transfers between devices: 195 us -> 179 us
  local copies, waits for them, and re-layouts: 37.8 us -> 46 us
  matrix products: 45.7 us -> 51.6 us
    all_to_all x1, waiting for transfers between devices: 56.8 us -> 40.2 us  [per_device(): lax.all_to_all(temporal_rows, 'seq', split_axis=1, concat_axis=0, tiled=T...]
    unnamed x27 -> x38, local copies, waits for them, and re-layouts: 2.15 us -> 10.8 us
    dot_general x1, matrix products: 3.02 us -> 6.69 us  [attend(): jnp.einsum('qhe,khe->hqk', query, keys, preferred_element_type=jnp.float32)]
  transfers between devices with their start and end apart: 5 -> 5, of which waited for: 3 -> 3; matrix products, arithmetic and copies ran while one was open for 24% -> 29% of each run, Pallas kernels for 0% -> 0%
where the time goes in v1:
time: 342 us; the launch traced here: 341 us
  waiting for transfers between devices  179 us (52%)
  matrix products  51.6 us (15%)
  local copies, waits for them, and re-layouts  46 us (13%)
  starting transfers between devices  24.5 us (7%)
  other arithmetic  14.5 us (4%)
  between operations  13.8 us (4%)
  blocking collectives  12.1 us (4%)
    all_gather x1, waiting for transfers between devices, per_device(): lax.all_gather(w_qkv, 'seq', axis=1, tiled=True)  131 us
    all_to_all x1, waiting for transfers between devices, per_device(): lax.all_to_all(temporal_rows, 'seq', split_axis=1, concat_axis=0, tiled=T...  40.2 us
    dot_general x1, matrix products, per_device(): jnp.dot(rows, lax.all_gather(w_qkv, 'seq', axis=1, tiled=True), preferred...  24.8 us
    all_to_all x1, starting transfers between devices, swap_blocks(): blocks = lax.all_to_all(blocks, name, split_axis=0, concat_axis=0)  12.4 us
    all_to_all x1, blocking collectives, per_device(): lax.all_to_all(both_halves.astype(jnp.bfloat16), 'seq', split_axis=0, con...  12.1 us
    unnamed x38, local copies, waits for them, and re-layouts  10.8 us
    convert_element_type x1, local copies, waits for them, and re-layouts, per_device(): projected = jnp.dot(rows, lax.all_gather(w_qkv, 'seq', axis=1, tiled=True...  8.91 us
    slice x2, local copies, waits for them, and re-layouts, per_device(): projected[:positions, :, SHEADS:].reshape(1, count, span, 3 * THEADS * HDIM)  8 us
  transfers between devices with their start and end apart: 5, of which 3 were waited for; matrix products, arithmetic and copies ran while one was open for 29% of the time, Pallas kernels for 0%

profile of v1, /device:TPU:0, one launch (start us, length us, event | category | flops | bytes accessed | tf_op | source)
XLA Modules:
  0.0 341.1 jit_solution(6613459880786389361)
XLA Ops:
  8.0 1.3 reduce
  9.4 0.8 reshape.111
  10.2 7.4 %all-to-all-start = ((bf16[16,2,1024]{2,1,0:T(2,128)(2,1)}), bf16[16,2,1024]{2,1,0:T(2,128)(2,1)S(1)}, u32[]{:S(2)}, u32[]{:S(2)}) async-start(bf16[16,2,1024]{2,1,0:T(2,128)(2,1)} %reshape.111), calls=%async_computation | async-start | bytes 131072 | tf_op jit(solution)/shard_map/all_to_all | solution.py:92
  18.4 2.1 fusion.51
  20.6 0.8 multiply_reduce_fusion.1
  21.8 3.3 add_convert_fusion.1
  25.0 131.1 %all-gather.3.cloned.1.call-done = bf16[3072,4608]{0,1:T(8,128)(2,1)} async-done(((bf16[3072,288]{0,1:T(8,128)(2,1)}), bf16[3072,4608]{0,1:T(8,128)(2,1)}) %all-gather.3.cloned.1.call-update) | async-done | bytes 28311568 | tf_op jit(solution)/shard_map/all_gather | solution.py:77
  156.1 24.8 %convolution_convert_fusion = bf16[640,4608]{1,0:T(8,128)(2,1)} fusion(bf16[3072,4608]{0,1:T(8,128)(2,1)} %all-gather.3.cloned.1.call-done, bf16[128,3072]{1,0:T(8,128)(2,1)S(1)} %dynamic-slice_bitcast_fusion, bf16[512,3072]{1,0:T(8,128)(2,1)} %add_convert_fusion.1), kind=kOutput, calls=%fused_computation | convolution fusion | flops 18130206720 | bytes 38141952 | tf_op jit(solution)/shard_map/dot_general | solution.py:76
  180.9 8.9 %copy.45 = bf16[640,4608]{0,1:T(8,128)(2,1)} copy(bf16[640,4608]{1,0:T(8,128)(2,1)} %convolution_convert_fusion) | data formatting | bytes 11796480 | tf_op jit(solution)/shard_map/convert_element_type | solution.py:78
  189.8 6.7 %fusion = (f32[6,512]{1,0:T(8,128)S(1)}, f32[6,512,640]{2,1,0:T(8,128)}) fusion(pred[640]{0:T(1024)(128)(4,1)S(1)} %concatenate.14, bf16[640,3,12,128]{0,3,2,1:T(8,128)(2,1)} %bitcast.160), kind=kOutput, calls=%fused_computation.3 | convolution fusion | flops 509211648 | bytes 9646720 | tf_op jit(solution)/shard_map/qhe,khe->hqk/dot_general | solution.py:29
  196.5 3.3 slice.78
  199.8 4.7 %copy.49 = bf16[512,3,6,128]{3,2,1,0:T(8,128)(2,1)} copy(bf16[512,3,6,128]{0,3,2,1:T(8,128)(2,1)} %slice.78) | data formatting | bytes 4718592 | tf_op jit(solution)/shard_map/slice | solution.py:85
  204.5 5.9 %reshape.104 = bf16[1,16,32,2304]{3,2,1,0:T(8,128)(2,1)} reshape(bf16[512,3,6,128]{3,2,1,0:T(8,128)(2,1)} %copy.49) | data formatting | bytes 4718592 | tf_op jit(solution)/shard_map/reshape | solution.py:85
  210.4 4.7 %all-to-all-start.2 = ((bf16[1,16,32,2304]{3,2,0,1:T(8,128)(2,1)}), bf16[1,16,32,2304]{3,2,0,1:T(8,128)(2,1)}, u32[]{:S(2)}, u32[]{:S(2)}) async-start(bf16[1,16,32,2304]{3,2,0,1:T(8,128)(2,1)} %bitcast.164), calls=%async_computation.2 | async-start | bytes 4718592 | tf_op jit(solution)/shard_map/all_to_all | solution.py:90
  215.1 4.4 %fusion.1 = f32[6,512]{1,0:T(8,128)S(1)} fusion(f32[6,512,640]{2,1,0:T(8,128)} %get-tuple-element.22, f32[6,512]{1,0:T(8,128)S(1)} %get-tuple-element.21, pred[640]{0:T(1024)(128)(4,1)S(1)} %concatenate.14), kind=kLoop, calls=%fused_computation.9 | loop fusion | flops 7861248 | bytes 7889536 | tf_op jit(solution)/shard_map/reduce_sum | solution.py:35
  219.5 5.6 %fusion.17 = bf16[512,6,128]{0,2,1:T(8,128)(2,1)S(1)} fusion(f32[6,512,640]{2,1,0:T(8,128)} %get-tuple-element.22, f32[6,512]{1,0:T(8,128)S(1)} %get-tuple-element.21, pred[640]{0:T(1024)(128)(4,1)S(1)} %concatenate.14, bf16[640,3,12,128]{0,3,2,1:T(8,128)(2,1)} %bitcast.162, f32[512,6]{0,1:T(8,128)S(1)} %bitcast.174), kind=kOutput, calls=%fused_computation.26 | convolution fusion | flops 511967232 | bytes 9659008 | tf_op jit(solution)/shard_map/hqk,khe->qhe/dot_general | solution.py:37
  225.9 0.9 reshape.103
  236.8 40.2 %all-to-all-done.2 = bf16[1,16,32,2304]{3,2,0,1:T(8,128)(2,1)} async-done(((bf16[1,16,32,2304]{3,2,0,1:T(8,128)(2,1)}), bf16[1,16,32,2304]{3,2,0,1:T(8,128)(2,1)}, u32[]{:S(2)}, u32[]{:S(2)}) %all-to-all-start.2) | async-done | bytes 2359328 | tf_op jit(solution)/shard_map/all_to_all | solution.py:90
  277.0 12.4 %all-to-all-start.1 = ((bf16[16,1,1,32,768]{4,3,2,1,0:T(8,128)(2,1)}), bf16[16,1,1,32,768]{4,3,2,1,0:T(8,128)(2,1)}, u32[]{:S(2)}, u32[]{:S(2)}) async-start(bf16[16,1,1,32,768]{4,3,2,1,0:T(8,128)(2,1)} %fusion.28), calls=%async_computation.1 | async-start | bytes 1572864 | tf_op jit(solution)/shard_map/all_to_all | solution.py:18
  289.4 0.8 fusion.26
  290.3 6.0 %reshape_reshape.7 = bf16[2,8,32,3,6,128]{5,4,3,2,1,0:T(8,128)(2,1)} reshape(bf16[1,16,32,2304]{3,2,0,1:T(8,128)(2,1)} %all-to-all-done.2) | data formatting | bytes 4718592 | tf_op jit(solution)/shard_map/reshape;reshape | solution.py:43
  296.4 2.4 fusion.48
  298.8 1.3 fusion.52
  300.7 1.1 fusion.16
  302.2 5.9 %all-to-all-done.1 = bf16[16,1,1,32,768]{4,3,2,1,0:T(8,128)(2,1)} async-done(((bf16[16,1,1,32,768]{4,3,2,1,0:T(8,128)(2,1)}), bf16[16,1,1,32,768]{4,3,2,1,0:T(8,128)(2,1)}, u32[]{:S(2)}, u32[]{:S(2)}) %all-to-all-start.1) | async-done | bytes 786464 | tf_op jit(solution)/shard_map/all_to_all | solution.py:18
  308.1 7.9 %fusion.12 = f32[512,3072]{1,0:T(8,128)S(1)} fusion(bf16[1536,3072]{0,1:T(8,128)(2,1)} %all-gather.5.cloned.1.call-done, bf16[512,768]{1,0:T(8,128)(2,1)S(1)} %bitcast.167, bf16[512,768]{1,0:T(8,128)(2,1)} %bitcast.33), kind=kOutput, calls=%fused_computation.19 | convolution fusion | flops 4834983936 | bytes 17301504 | tf_op jit(solution)/shard_map/dot_general | solution.py:102
  316.1 1.0 fusion.53
  317.1 0.8 multiply_reduce_fusion
  318.0 1.6 add_convert_fusion
  319.7 1.1 convolution_convert_fusion.1
  321.2 12.1 %all_to_all.32 = bf16[16,2,1024]{2,1,0:T(2,128)(2,1)S(1)} all-to-all(bf16[16,2,1024]{2,1,0:T(2,128)(2,1)S(1)} %reshape.113), channel_id=1, replica_groups=mesh['groups'=2,'seq'=16] {'seq'}, dimensions={0} | all-to-all | bytes 131072 | tf_op jit(solution)/shard_map/all_to_all | solution.py:126
  333.4 0.9 reshape.107
  (66 shorter events, 15.3 us)
Async XLA Ops:
  6.5 14.8 %copy-start = (bf16[2,128,3072]{2,1,0:T(8,128)(2,1)S(1)}, bf16[2,128,3072]{2,1,0:T(8,128)(2,1)}, u32[]{:S(2)}) copy-start(bf16[2,128,3072]{2,1,0:T(8,128)(2,1)} %param.9) | copy-start | bytes 4718596
  6.5 149.5 %all-gather.3.cloned.1.call-start = ((), (), s32[]{:S(2)}) async-start(), calls=%async_computation.4 | async-start | bytes 30081024 | tf_op jit(solution)/shard_map/all_gather | solution.py:77
  7.3 295.0 %all-gather.5.cloned.1.call-start = ((), (), s32[]{:S(2)}) async-start(), calls=%async_computation.5 | async-start | bytes 10027008 | tf_op jit(solution)/shard_map/all_gather | solution.py:104
  10.2 200.3 %all-to-all-start = ((bf16[16,2,1024]{2,1,0:T(2,128)(2,1)}), bf16[16,2,1024]{2,1,0:T(2,128)(2,1)S(1)}, u32[]{:S(2)}, u32[]{:S(2)}) async-start(bf16[16,2,1024]{2,1,0:T(2,128)(2,1)} %reshape.111), calls=%async_computation | async-start | bytes 131072 | tf_op jit(solution)/shard_map/all_to_all | solution.py:92
  18.4 2.9 copy-start.8
  210.4 9.1 %copy-start.6 = (bf16[16,2,1024]{2,1,0:T(2,128)(2,1)}, bf16[16,2,1024]{2,1,0:T(2,128)(2,1)S(1)}, u32[]{:S(2)}) copy-start(bf16[16,2,1024]{2,1,0:T(2,128)(2,1)S(1)} %all-to-all-done) | copy-start | bytes 196612
  210.4 66.6 %all-to-all-start.2 = ((bf16[1,16,32,2304]{3,2,0,1:T(8,128)(2,1)}), bf16[1,16,32,2304]{3,2,0,1:T(8,128)(2,1)}, u32[]{:S(2)}, u32[]{:S(2)}) async-start(bf16[1,16,32,2304]{3,2,0,1:T(8,128)(2,1)} %bitcast.164), calls=%async_computation.2 | async-start | bytes 4718592 | tf_op jit(solution)/shard_map/all_to_all | solution.py:90
  225.2 65.0 %copy-start.7 = (bf16[16,2,1024]{2,1,0:T(2,128)(2,1)S(1)}, bf16[16,2,1024]{2,1,0:T(2,128)(2,1)}, u32[]{:S(2)}) copy-start(bf16[16,2,1024]{2,1,0:T(2,128)(2,1)} %copy-done.6) | copy-start | bytes 196612
  277.0 31.1 %all-to-all-start.1 = ((bf16[16,1,1,32,768]{4,3,2,1,0:T(8,128)(2,1)}), bf16[16,1,1,32,768]{4,3,2,1,0:T(8,128)(2,1)}, u32[]{:S(2)}, u32[]{:S(2)}) async-start(bf16[16,1,1,32,768]{4,3,2,1,0:T(8,128)(2,1)} %fusion.28), calls=%async_computation.1 | async-start | bytes 1572864 | tf_op jit(solution)/shard_map/all_to_all | solution.py:18
  308.1 7.9 %copy-start.2 = (bf16[64,3072]{1,0:T(8,128)(2,1)S(1)}, bf16[64,3072]{1,0:T(8,128)(2,1)}, u32[]{:S(2)}) copy-start(bf16[64,3072]{1,0:T(8,128)(2,1)} %param.12) | copy-start | bytes 1179652
  308.1 7.9 %copy-start.4 = (f32[16,3072]{1,0:T(8,128)S(1)}, f32[16,3072]{1,0:T(8,128)}, u32[]{:S(2)}) copy-start(f32[16,3072]{1,0:T(8,128)} %get-tuple-element.10) | copy-start | bytes 589828
  317.1 0.9 copy-start.3
  317.9 1.8 copy-start.5
  317.9 16.4 %copy-start.1 = (bf16[2,128,3072]{2,1,0:T(8,128)(2,1)S(1)}, bf16[2,128,3072]{2,1,0:T(8,128)(2,1)}, u32[]{:S(2)}) copy-start(bf16[2,128,3072]{2,1,0:T(8,128)(2,1)} %param.9) | copy-start | bytes 4718596
Sparse Core Ops, SparseCore 0:
  8.9 147.1 all-gather.2
  158.4 111.9 all-gather.4
